TPU v7x, 32 devices: a whole 2x2x4 slice. The times are simulated.
32 devices in a mesh: dom: 16 (over z, y, x), blk: 2 (over core).
Axes of the slice: x: 2, y: 2, z: 4, core: 2. Of those that a mesh axis runs over, the one named last changes fastest.
Arguments:
- self_block: float32 [96, 96, 4096], P(None, None, ('dom', 'blk')), may hold values from -1 to 8
- couple: float32 [64, 96, 4096], P(None, None, ('dom', 'blk')), may hold values from -0.625 to 0.625
- inverse: float32 [64, 64, 4096], P(None, None, ('dom', 'blk')), may hold values from -1 to 8
- body_force: float32 [3, 64, 4096], P(None, None, ('dom', 'blk')), may hold values from -6 to 6
- face_mortar: int32 [24576], P(('dom', 'blk')), may hold values from 0 to 8191, as said below
- face_kind: int32 [24576], P(('dom', 'blk')), may hold values from 0 to 4
Outputs:
- trace_field: float32 [48, 8192], P(None, ('dom', 'blk'))
- interior: float32 [3, 64, 4096], P(None, None, ('dom', 'blk'))
Inputs may be any that keep to these rules, and one draw needn't show every extreme that they name: `face_mortar`: mortar m is owned by device m // 256 along the curve. The 768 slots of device r come in five runs in this order: mortars owned by r - 2, r - 1, r, r + 1, r + 32 // 2 (modulo 32); each of the four other runs holds 1 to 32 slots and one of them holds exactly 32; the first 256 slots of the run owned by r name each of r's mortars once.
All inputs are finite; a program needn't handle non-finite values.
Results may differ from a plain program's by a relative error of at most 0.0003.
Values sent between devices are 32-bit elements; how exact they have to be, the bound alone decides.
No kernel may reach another device: no remote copies, remote signals or barrier semaphores. Data moves between devices by JAX's collectives and lax.ppermute only.
A program may use at most 128 MiB of HBM per device.

v0:
```python
import jax
import jax.numpy as jnp
import numpy as np
from jax import lax
from jax.sharding import PartitionSpec as P

ITERS = 3
PRECISE = lax.Precision.HIGHEST


def near_offsets(ranks):
    return (-2, -1, 1, ranks // 2)


def interp_tables():
    abscissae = -np.cos(np.pi * np.arange(4) / 3.0)

    def lagrange(points):
        columns = [
            np.prod(
                [
                    (points - abscissae[other_node])
                    / (abscissae[basis_node] - abscissae[other_node])
                    for other_node in range(4)
                    if other_node != basis_node
                ],
                axis=0,
            )
            for basis_node in range(4)
        ]
        return np.stack(columns, axis=1)

    lower_map = lagrange((abscissae - 1.0) / 2.0)
    upper_map = lagrange((abscissae + 1.0) / 2.0)
    identity = np.eye(4)
    return np.stack(
        [
            np.kron(identity, identity),
            np.kron(lower_map, lower_map),
            np.kron(lower_map, upper_map),
            np.kron(upper_map, lower_map),
            np.kron(upper_map, upper_map),
        ]
    )


def to_faces(values, kind_ids, tables):
    node_count = tables.shape[1]
    by_comp = values.reshape(values.shape[0] // node_count, node_count, values.shape[1])
    mapped = jnp.einsum("kab,cbi->kcai", tables, by_comp, precision=PRECISE)
    selector = (kind_ids[None, :] == jnp.arange(5, dtype=jnp.int32)[:, None]).astype(values.dtype)
    return jnp.einsum("kcai,ki->cai", mapped, selector, precision=PRECISE).reshape(values.shape)


def to_mortar(values, kind_ids, tables):
    node_count = tables.shape[1]
    by_comp = values.reshape(values.shape[0] // node_count, node_count, values.shape[1])
    mapped = jnp.einsum("kab,cai->kcbi", tables, by_comp, precision=PRECISE)
    selector = (kind_ids[None, :] == jnp.arange(5, dtype=jnp.int32)[:, None]).astype(values.dtype)
    return jnp.einsum("kcbi,ki->cbi", mapped, selector, precision=PRECISE).reshape(values.shape)


def slot_to_element(values, elements, node_count):
    comp_count = values.shape[0] // node_count
    arranged = values.reshape(comp_count, node_count, elements, 6)
    return jnp.transpose(arranged, (0, 3, 1, 2)).reshape(comp_count, 6 * node_count, elements)


def element_to_slot(values, elements, node_count):
    comp_count = values.shape[0]
    arranged = values.reshape(comp_count, 6, node_count, elements)
    return jnp.transpose(arranged, (0, 2, 3, 1)).reshape(comp_count * node_count, elements * 6)


def to_owners(buffer):
    result = lax.all_to_all(buffer, ("dom", "blk"), split_axis=1, concat_axis=1, tiled=True)
    return result


def to_elements(buffer):
    result = lax.all_to_all(buffer, ("dom", "blk"), split_axis=1, concat_axis=1, tiled=True)
    return result


def local(self_block, couple, inverse, body_force, face_mortar, face_kind):
    elements = self_block.shape[2]
    owned = 2 * elements
    capacity = max(2, elements // 4)
    ranks = lax.axis_size(("dom", "blk"))
    offsets_list = near_offsets(ranks)
    my_rank = lax.axis_index(("dom", "blk"))
    tables = jnp.asarray(interp_tables(), dtype=jnp.float32)
    node_count = tables.shape[1]
    owner_rank = face_mortar // owned
    local_index = face_mortar % owned
    distance = (owner_rank - my_rank) % ranks
    offset = jnp.where(distance > ranks // 2, distance - ranks, distance)
    is_self = offset == 0
    slot_ids = jnp.arange(face_mortar.shape[0], dtype=jnp.int32)
    run_start = jnp.zeros_like(slot_ids)
    run_block = jnp.zeros_like(slot_ids)
    for number in range(len(offsets_list)):
        shift_by = offsets_list[number]
        inside = offset == shift_by
        run_start = jnp.where(inside, jnp.sum((offset < shift_by).astype(jnp.int32)), run_start)
        run_block = jnp.where(inside, number, run_block)
    position = slot_ids - run_start
    buffer_width = ranks * capacity
    target = (my_rank + offset) % ranks * capacity + position
    target = jnp.where(is_self, buffer_width, target)
    sent_index = (
        jnp.full((buffer_width + 1,), owned, jnp.int32).at[target].set(local_index)[:buffer_width]
    )
    readers = lax.all_to_all(sent_index, ("dom", "blk"), split_axis=0, concat_axis=0, tiled=True)
    all_index = jnp.concatenate([jnp.where(is_self, local_index, owned), readers])
    column = jnp.where(is_self, local_index, owned + target)

    def assemble(per_element):
        slot_values = element_to_slot(per_element, elements, node_count)
        mortar_values = to_mortar(slot_values, face_kind, tables)
        outgoing = (
            jnp.zeros((mortar_values.shape[0], buffer_width + 1), jnp.float32)
            .at[:, target]
            .set(mortar_values)[:, :buffer_width]
        )
        received = to_owners(outgoing)
        stacked = jnp.concatenate([mortar_values, received], axis=1)
        return (
            jnp.zeros((mortar_values.shape[0], owned + 1), jnp.float32)
            .at[:, all_index]
            .add(stacked)[:, :owned]
        )

    def spread(field_values):
        padded = jnp.concatenate(
            [field_values, jnp.zeros((field_values.shape[0], 1), jnp.float32)], axis=1
        )
        received = to_elements(padded[:, readers])
        source = jnp.concatenate([field_values, received], axis=1)
        return slot_to_element(to_faces(source[:, column], face_kind, tables), elements, node_count)

    solved_load = jnp.einsum("ike,cke->cie", inverse, body_force, precision=PRECISE)
    local_rhs = jnp.einsum("iae,cie->cae", couple, solved_load, precision=PRECISE)
    residual = assemble(local_rhs)
    weighted = jnp.einsum("ike,kbe->ibe", inverse, couple, precision=PRECISE)
    condensed = self_block + jnp.einsum("iae,ibe->abe", couple, weighted, precision=PRECISE)
    trace_field = jnp.zeros_like(residual)
    direction = residual
    current = lax.psum(jnp.sum(residual * residual), ("dom", "blk"))
    for iteration in range(ITERS):
        image_field = assemble(
            jnp.einsum("abe,cbe->cae", condensed, spread(direction), precision=PRECISE)
        )
        curve_sum, cross_sum, image_sum = lax.psum(
            (
                jnp.sum(direction * image_field),
                jnp.sum(residual * image_field),
                jnp.sum(image_field * image_field),
            ),
            ("dom", "blk"),
        )
        step_length = current / curve_sum
        trace_field = trace_field + step_length * direction
        if iteration + 1 < ITERS:
            residual = residual - step_length * image_field
            following = (
                current - 2.0 * step_length * cross_sum + step_length * step_length * image_sum
            )
            direction = residual + following / current * direction
            current = following
    faces_elem = spread(trace_field)
    difference = body_force - jnp.einsum("ibe,cbe->cie", couple, faces_elem, precision=PRECISE)
    interior = jnp.einsum("ike,cke->cie", inverse, difference, precision=PRECISE)
    return (trace_field, interior)


def solution(mesh):
    placed = (
        P(None, None, ("dom", "blk")),
        P(None, None, ("dom", "blk")),
        P(None, None, ("dom", "blk")),
        P(None, None, ("dom", "blk")),
        P(("dom", "blk")),
        P(("dom", "blk")),
    )
    return jax.shard_map(
        local,
        mesh=mesh,
        in_specs=placed,
        out_specs=(P(None, ("dom", "blk")), P(None, None, ("dom", "blk"))),
        check_vma=False,
    )
```

profile of v0, /device:TPU:1, one launch (start us, length us, event | category | flops | bytes accessed | tf_op | source)
XLA Modules:
  0.0 478.3 jit_solution(3439235943275158686)
XLA Ops:
  0.6 1.6 convert_reduce_fusion.3
  2.3 3.2 compare_select_fusion.2
  5.5 3.4 scatter_custom_fusion
  9.6 7.1 %all-to-all-start = ((s32[32,32,1]{1,2,0:T(1,128)}), s32[32,32,1]{1,2,0:T(1,128)S(1)}, u32[]{:S(2)}, u32[]{:S(2)}) async-start(s32[32,32,1]{1,2,0:T(1,128)} %bitcast.16), calls=%async_computation | async-start | bytes 32768 | tf_op jit(solution)/shard_map/all_to_all | solution.py:114
  18.4 5.1 %copy.378 = f32[64,96,128]{1,0,2:T(8,128)} copy(f32[64,96,128]{2,1,0:T(8,128)} %param.8) | data formatting | bytes 6291456 | tf_op args[1]
  23.5 4.5 copy.377
  28.0 8.5 %convolution_bitcast_fusion.14 = f32[3,64,128]{1,0,2:T(4,128)S(1)} fusion(f32[3,64,128]{1,0,2:T(4,128)S(1)} %copy.376, f32[64,64,128]{1,0,2:T(8,128)} %copy.377), kind=kOutput, calls=%fused_computation.55 | convolution fusion | flops 18874368 | bytes 2293760 | tf_op jit(solution)/shard_map/ike,cke->cie/dot_general | solution.py:142
  36.5 7.2 %fusion.54 = f32[128,96,64]{1,2,0:T(8,128)} fusion(f32[64,96,128]{1,0,2:T(8,128)S(1)} %copy-done, f32[64,64,128]{1,0,2:T(8,128)} %copy.377), kind=kOutput, calls=%fused_computation.135 | convolution fusion | flops 603979776 | bytes 8388608 | tf_op jit(solution)/shard_map/ike,kbe->ibe/dot_general | solution.py:145
  43.6 3.7 convolution_bitcast_fusion.13
  48.2 14.5 %fusion = f32[128,96,96]{2,1,0:T(8,128)} fusion(f32[64,96,128]{1,0,2:T(8,128)} %copy.378, f32[128,96,64]{1,2,0:T(8,128)} %fusion.54), kind=kOutput, calls=%fused_computation.18 | convolution fusion | flops 905969664 | bytes 11010048 | tf_op jit(solution)/shard_map/iae,ibe->abe/dot_general | solution.py:146
  64.3 4.3 scatter_custom_fusion.1
  69.8 6.3 %copy.393 = f32[128,96,96]{0,1,2:T(8,128)} copy(f32[128,96,96]{2,1,0:T(8,128)} %fusion) | data formatting | bytes 9437184 | tf_op jit(solution)/shard_map/iae,ibe->abe/dot_general | solution.py:146
  76.1 5.8 %all-to-all-start.1 = ((f32[32,1,1536]{2,1,0:T(1,128)}), f32[32,1,1536]{2,1,0:T(1,128)S(1)}, u32[]{:S(2)}, u32[]{:S(2)}) async-start(f32[32,1,1536]{2,1,0:T(1,128)} %reshape.401), calls=%async_computation.1 | async-start | bytes 393216 | tf_op jit(solution)/shard_map/all_to_all | solution.py:76
  83.3 7.9 %all-to-all-done.1 = f32[32,1,1536]{2,1,0:T(1,128)S(1)} async-done(((f32[32,1,1536]{2,1,0:T(1,128)}), f32[32,1,1536]{2,1,0:T(1,128)S(1)}, u32[]{:S(2)}, u32[]{:S(2)}) %all-to-all-start.1) | async-done | bytes 196640 | tf_op jit(solution)/shard_map/all_to_all | solution.py:76
  93.6 13.1 %scatter_custom_fusion.2 = f32[48,257]{0,1:T(8,128)S(1)} fusion(s32[1792]{0:T(1024)S(1)} %fusion.42, f32[1792,48]{1,0:T(8,128)S(1)} %copy.384, f32[]{:T(128)} %constant.68.clone.1), kind=kCustom, calls=%fused_computation.91 | custom fusion | flops 86016 | bytes 49348 | tf_op jit(solution)/shard_map/scatter-add | solution.py:131
  106.8 2.8 gather_fusion
  110.9 2.7 all-to-all-start.2
  113.5 7.0 %bitcast_add_fusion = f32[96,96,128]{2,1,0:T(8,128)} fusion(f32[96,96,128]{2,1,0:T(8,128)} %param.7, f32[128,96,96]{0,1,2:T(8,128)} %copy.393), kind=kLoop, calls=%fused_computation.17 | loop fusion | flops 1179648 | bytes 14155776 | tf_op jit(solution)/shard_map/add | solution.py:146
  120.5 6.3 %copy.395 = f32[96,96,128]{1,0,2:T(8,128)} copy(f32[96,96,128]{2,1,0:T(8,128)} %bitcast_add_fusion) | data formatting | bytes 9437184 | tf_op jit(solution)/shard_map/add | solution.py:146
  128.2 1.6 gather_fusion.1
  131.8 11.8 %convolution_bitcast_fusion.12 = f32[3,96,128]{1,0,2:T(4,128)S(1)} fusion(f32[3,96,128]{1,0,2:T(4,128)S(1)} %copy.394, f32[96,96,128]{1,0,2:T(8,128)} %copy.395), kind=kOutput, calls=%fused_computation.53 | convolution fusion | flops 42467328 | bytes 5013504 | tf_op jit(solution)/shard_map/abe,cbe->cae/dot_general | solution.py:152
  144.5 1.4 fusion.16
  146.1 4.3 scatter_custom_fusion.3
  150.9 15.3 %all_to_all.105 = f32[32,1,1536]{2,1,0:T(1,128)S(1)} all-to-all(f32[32,1,1536]{2,1,0:T(1,128)S(1)} %reshape.405), channel_id=1, replica_groups=mesh['dom'=16,'blk'=2] {'dom','blk'}, dimensions={0} | all-to-all | bytes 393216 | tf_op jit(solution)/shard_map/all_to_all | solution.py:76
  168.0 13.1 %scatter_custom_fusion.4 = f32[48,257]{0,1:T(8,128)S(1)} fusion(s32[1792]{0:T(1024)S(1)} %fusion.42, f32[1792,48]{1,0:T(8,128)S(1)} %copy.401, f32[]{:T(128)} %constant.68.clone.1), kind=kCustom, calls=%fused_computation.88 | custom fusion | flops 86016 | bytes 49348 | tf_op jit(solution)/shard_map/scatter-add | solution.py:131
  181.9 37.7 %all-reduce.4 = (f32[]{:T(128)}, f32[]{:T(128)}, f32[]{:T(128)}) all-reduce(f32[]{:T(128)} %get-tuple-element.23, f32[]{:T(128)} %get-tuple-element.22, f32[]{:T(128)} %get-tuple-element.21), channel_id=1, replica_groups=mesh['dom'=16,'blk'=2] {'dom','blk'}, use_global_device_ids=true, to_apply=%region_8.9 | all-reduce | flops 3 | bytes 24 | tf_op jit(solution)/shard_map/psum | solution.py:149
  223.5 2.8 gather_fusion.2
  226.9 13.9 %all_to_all.106 = f32[32,1,1536]{2,1,0:T(1,128)S(1)} all-to-all(f32[32,1,1536]{2,1,0:T(1,128)S(1)} %reshape.407), channel_id=1, replica_groups=mesh['dom'=16,'blk'=2] {'dom','blk'}, dimensions={0} | all-to-all | bytes 393216 | tf_op jit(solution)/shard_map/all_to_all | solution.py:81
  242.2 1.6 gather_fusion.3
  245.8 11.8 %convolution_bitcast_fusion.11 = f32[3,96,128]{1,0,2:T(4,128)S(1)} fusion(f32[3,96,128]{1,0,2:T(4,128)S(1)} %copy.407, f32[96,96,128]{1,0,2:T(8,128)} %copy.395), kind=kOutput, calls=%fused_computation.52 | convolution fusion | flops 42467328 | bytes 5013504 | tf_op jit(solution)/shard_map/abe,cbe->cae/dot_general | solution.py:152
  260.1 4.3 scatter_custom_fusion.5
  264.9 11.6 %all_to_all.107 = f32[32,1,1536]{2,1,0:T(1,128)S(1)} all-to-all(f32[32,1,1536]{2,1,0:T(1,128)S(1)} %reshape.409), channel_id=1, replica_groups=mesh['dom'=16,'blk'=2] {'dom','blk'}, dimensions={0} | all-to-all | bytes 393216 | tf_op jit(solution)/shard_map/all_to_all | solution.py:76
  278.3 13.1 %scatter_custom_fusion.6 = f32[48,257]{0,1:T(8,128)S(1)} fusion(s32[1792]{0:T(1024)S(1)} %fusion.42, f32[1792,48]{1,0:T(8,128)S(1)} %copy.414, f32[]{:T(128)} %constant.68.clone.1), kind=kCustom, calls=%fused_computation.86 | custom fusion | flops 86016 | bytes 49348 | tf_op jit(solution)/shard_map/scatter-add | solution.py:131
  292.2 37.7 %all-reduce.3 = (f32[]{:T(128)}, f32[]{:T(128)}, f32[]{:T(128)}) all-reduce(f32[]{:T(128)} %get-tuple-element.20, f32[]{:T(128)} %get-tuple-element.19, f32[]{:T(128)} %get-tuple-element.18), channel_id=1, replica_groups=mesh['dom'=16,'blk'=2] {'dom','blk'}, use_global_device_ids=true, to_apply=%region_18.19 | all-reduce | flops 3 | bytes 24 | tf_op jit(solution)/shard_map/psum | solution.py:154
  332.0 2.8 gather_fusion.4
  335.3 13.9 %all_to_all.108 = f32[32,1,1536]{2,1,0:T(1,128)S(1)} all-to-all(f32[32,1,1536]{2,1,0:T(1,128)S(1)} %reshape.411), channel_id=1, replica_groups=mesh['dom'=16,'blk'=2] {'dom','blk'}, dimensions={0} | all-to-all | bytes 393216 | tf_op jit(solution)/shard_map/all_to_all | solution.py:81
  350.7 1.6 gather_fusion.5
  354.2 11.8 %convolution_bitcast_fusion.10 = f32[3,96,128]{1,0,2:T(4,128)S(1)} fusion(f32[3,96,128]{1,0,2:T(4,128)S(1)} %copy.420, f32[96,96,128]{1,0,2:T(8,128)} %copy.395), kind=kOutput, calls=%fused_computation.51 | convolution fusion | flops 42467328 | bytes 5013504 | tf_op jit(solution)/shard_map/abe,cbe->cae/dot_general | solution.py:152
  368.5 4.3 scatter_custom_fusion.7
  373.3 11.6 %all_to_all.109 = f32[32,1,1536]{2,1,0:T(1,128)S(1)} all-to-all(f32[32,1,1536]{2,1,0:T(1,128)S(1)} %reshape.413), channel_id=1, replica_groups=mesh['dom'=16,'blk'=2] {'dom','blk'}, dimensions={0} | all-to-all | bytes 393216 | tf_op jit(solution)/shard_map/all_to_all | solution.py:76
  386.8 13.1 %scatter_custom_fusion.8 = f32[48,257]{0,1:T(8,128)S(1)} fusion(s32[1792]{0:T(1024)S(1)} %fusion.42, f32[1792,48]{1,0:T(8,128)S(1)} %copy.427, f32[]{:T(128)} %constant.68.clone.1), kind=kCustom, calls=%fused_computation.84 | custom fusion | flops 86016 | bytes 49348 | tf_op jit(solution)/shard_map/scatter-add | solution.py:131
  400.6 37.6 %psum.58 = f32[]{:T(128)} all-reduce(f32[]{:T(128)} %fusion.31), channel_id=1, replica_groups=mesh['dom'=16,'blk'=2] {'dom','blk'}, use_global_device_ids=true, to_apply=%region_26.27 | all-reduce | flops 1 | bytes 8 | tf_op jit(solution)/shard_map/psum | solution.py:154
  438.9 2.8 gather_fusion.6
  442.9 4.9 %all-to-all-start.8 = ((f32[32,1,1536]{2,1,0:T(1,128)}), f32[32,1,1536]{2,1,0:T(1,128)S(1)}, u32[]{:S(2)}, u32[]{:S(2)}) async-start(f32[32,1,1536]{2,1,0:T(1,128)} %reshape.415), calls=%async_computation.8 | async-start | bytes 393216 | tf_op jit(solution)/shard_map/all_to_all | solution.py:81
  448.5 8.5 %all-to-all-done.8 = f32[32,1,1536]{2,1,0:T(1,128)S(1)} async-done(((f32[32,1,1536]{2,1,0:T(1,128)}), f32[32,1,1536]{2,1,0:T(1,128)S(1)}, u32[]{:S(2)}, u32[]{:S(2)}) %all-to-all-start.8) | async-done | bytes 196640 | tf_op jit(solution)/shard_map/all_to_all | solution.py:81
  458.5 1.6 gather_fusion.7
  462.1 8.5 %fusion.22 = f32[3,64,128]{1,0,2:T(4,128)S(1)} fusion(f32[3,64,128]{1,0,2:T(4,128)S(1)} %copy-done.4, f32[3,96,128]{1,0,2:T(4,128)S(1)} %copy.433, f32[64,96,128]{1,0,2:T(8,128)} %copy.378), kind=kOutput, calls=%fused_computation.50 | convolution fusion | flops 28336128 | bytes 3489792 | tf_op jit(solution)/shard_map/ibe,cbe->cie/dot_general | solution.py:172
  470.6 6.6 %convolution_bitcast_fusion.8 = f32[3,64,128]{1,0,2:T(4,128)S(1)} fusion(f32[3,64,128]{1,0,2:T(4,128)S(1)} %fusion.22, f32[64,64,128]{1,0,2:T(8,128)S(1)} %copy-done.1), kind=kOutput, calls=%fused_computation.48 | convolution fusion | flops 18874368 | bytes 2293760 | tf_op jit(solution)/shard_map/ike,cke->cie/dot_general | solution.py:173
  (128 shorter events, 43.2 us)
Async XLA Ops:
  0.6 22.9 %copy-start.5 = (f32[64,64,128]{2,1,0:T(8,128)S(1)}, f32[64,64,128]{2,1,0:T(8,128)}, u32[]{:S(2)}) copy-start(f32[64,64,128]{2,1,0:T(8,128)} %param.9) | copy-start | bytes 6291460
  9.6 66.6 %all-to-all-start = ((s32[32,32,1]{1,2,0:T(1,128)}), s32[32,32,1]{1,2,0:T(1,128)S(1)}, u32[]{:S(2)}, u32[]{:S(2)}) async-start(s32[32,32,1]{1,2,0:T(1,128)} %bitcast.16), calls=%async_computation | async-start | bytes 32768 | tf_op jit(solution)/shard_map/all_to_all | solution.py:114
  18.4 9.6 %copy-start.3 = (f32[3,64,128]{1,0,2:T(4,128)}, f32[3,64,128]{1,0,2:T(4,128)S(1)}, u32[]{:S(2)}) copy-start(f32[3,64,128]{1,0,2:T(4,128)S(1)} %copy.376) | copy-start | bytes 294916
  28.0 8.5 %copy-start = (f32[64,96,128]{1,0,2:T(8,128)S(1)}, f32[64,96,128]{1,0,2:T(8,128)}, u32[]{:S(2)}) copy-start(f32[64,96,128]{1,0,2:T(8,128)} %copy.378) | copy-start | bytes 9437188
  48.2 14.5 %copy-start.2 = (f32[5,16,16,1]{1,2,0,3:T(8,128)S(1)}, f32[5,16,16,1]{1,2,0,3:T(8,128)}, u32[]{:S(2)}) copy-start(f32[5,16,16,1]{1,2,0,3:T(8,128)} %constant.104) | copy-start | bytes 15364
  76.1 30.6 %copy-start.6 = (pred[257]{0:T(512)(128)(4,1)S(1)}, pred[257]{0:T(512)(128)(4,1)}, u32[]{:S(2)}) copy-start(pred[257]{0:T(512)(128)(4,1)} %constant.86.clone.1) | copy-start | bytes 775
  76.1 15.1 %all-to-all-start.1 = ((f32[32,1,1536]{2,1,0:T(1,128)}), f32[32,1,1536]{2,1,0:T(1,128)S(1)}, u32[]{:S(2)}, u32[]{:S(2)}) async-start(f32[32,1,1536]{2,1,0:T(1,128)} %reshape.401), calls=%async_computation.1 | async-start | bytes 393216 | tf_op jit(solution)/shard_map/all_to_all | solution.py:76
  110.9 15.9 %all-to-all-start.2 = ((f32[32,1,1536]{2,1,0:T(1,128)}), f32[32,1,1536]{2,1,0:T(1,128)S(1)}, u32[]{:S(2)}, u32[]{:S(2)}) async-start(f32[32,1,1536]{2,1,0:T(1,128)} %reshape.403), calls=%async_computation.2 | async-start | bytes 393216 | tf_op jit(solution)/shard_map/all_to_all | solution.py:81
  442.9 14.1 %all-to-all-start.8 = ((f32[32,1,1536]{2,1,0:T(1,128)}), f32[32,1,1536]{2,1,0:T(1,128)S(1)}, u32[]{:S(2)}, u32[]{:S(2)}) async-start(f32[32,1,1536]{2,1,0:T(1,128)} %reshape.415), calls=%async_computation.8 | async-start | bytes 393216 | tf_op jit(solution)/shard_map/all_to_all | solution.py:81
  458.5 3.6 copy-start.4
  462.1 8.5 %copy-start.1 = (f32[64,64,128]{1,0,2:T(8,128)S(1)}, f32[64,64,128]{1,0,2:T(8,128)}, u32[]{:S(2)}) copy-start(f32[64,64,128]{1,0,2:T(8,128)} %copy.377) | copy-start | bytes 6291460
where the time goes:
time: 488 us; the launch traced here: 478 us
  blocking collectives  179 us (37%)
  matrix products  93.1 us (19%)
  local copies, waits for them, and re-layouts  83.2 us (17%)
  other arithmetic  77.3 us (16%)
  starting transfers between devices  20.5 us (4%)
  waiting for transfers between devices  16.4 us (3%)
  between operations  8.46 us (2%)
    psum x2, blocking collectives, local(): lax.psum((jnp.sum(direction * image_field), jnp.sum(residual * image_fiel...  75.3 us
    scatter-add x4, other arithmetic, assemble(): return jnp.zeros((mortar_values.shape[0], owned + 1), jnp.float32).at[:,...  52.6 us
    all_to_all x3, blocking collectives, to_owners(): lax.all_to_all(buffer, ('dom', 'blk'), split_axis=1, concat_axis=1, tiled...  38.5 us
    psum x1, blocking collectives, local(): current = lax.psum(jnp.sum(residual * residual), ('dom', 'blk'))  37.7 us
    dot_general x3, matrix products, local(): jnp.einsum('abe,cbe->cae', condensed, spread(direction), precision=PRECISE)  35.5 us
    all_to_all x2, blocking collectives, to_elements(): lax.all_to_all(buffer, ('dom', 'blk'), split_axis=1, concat_axis=1, tiled...  27.9 us
    unnamed x36, local copies, waits for them, and re-layouts  20 us
    scatter x4, local copies, waits for them, and re-layouts, assemble(): outgoing = jnp.zeros((mortar_values.shape[0], buffer_width + 1), jnp.floa...  17.1 us
  transfers between devices with their start and end apart: 4, of which 2 were waited for; matrix products, arithmetic and copies ran while one was open for 16% of the time, Pallas kernels for 0%

commit v1 on v0

--- a/solution.py
+++ b/solution.py
@@ -152,12 +152,15 @@
             jnp.einsum("abe,cbe->cae", condensed, spread(direction), precision=PRECISE)
         )
         curve_sum, cross_sum, image_sum = lax.psum(
-            (
-                jnp.sum(direction * image_field),
-                jnp.sum(residual * image_field),
-                jnp.sum(image_field * image_field),
+            lax.psum(
+                (
+                    jnp.sum(direction * image_field),
+                    jnp.sum(residual * image_field),
+                    jnp.sum(image_field * image_field),
+                ),
+                "blk",
             ),
-            ("dom", "blk"),
+            "dom",
         )
         step_length = current / curve_sum
         trace_field = trace_field + step_length * direction

time: 488 us -> 533 us (1.092)
  blocking collectives: 179 us -> 220 us
    psum x0 -> x3, blocking collectives: none -> 97.3 us  [local(): lax.psum(lax.psum((jnp.sum(direction * image_field), jnp.sum(residual * i...]
    psum x2 -> x3, blocking collectives: 75.3 us -> 10.3 us  [local(): lax.psum((jnp.sum(direction * image_field), jnp.sum(residual * image_fiel...]
    all_to_all x2, blocking collectives: 27.9 us -> 36.5 us  [to_elements(): lax.all_to_all(buffer, ('dom', 'blk'), split_axis=1, concat_axis=1, tiled...]
  transfers between devices with their start and end apart: 4 -> 4, of which waited for: 2 -> 2; matrix products, arithmetic and copies ran while one was open for 16% -> 14% of each run, Pallas kernels for 0% -> 0%
where the time goes in v1:
time: 533 us; the launch traced here: 524 us
  blocking collectives  220 us (41%)
  matrix products  93.1 us (17%)
  local copies, waits for them, and re-layouts  83.2 us (16%)
  other arithmetic  77.3 us (15%)
  starting transfers between devices  25.3 us (5%)
  waiting for transfers between devices  16.6 us (3%)
  between operations  8.29 us (2%)
    psum x3, blocking collectives, local(): lax.psum(lax.psum((jnp.sum(direction * image_field), jnp.sum(residual * i...  97.3 us
    scatter-add x4, other arithmetic, assemble(): return jnp.zeros((mortar_values.shape[0], owned + 1), jnp.float32).at[:,...  52.6 us
    all_to_all x3, blocking collectives, to_owners(): lax.all_to_all(buffer, ('dom', 'blk'), split_axis=1, concat_axis=1, tiled...  38.3 us
    psum x1, blocking collectives, local(): current = lax.psum(jnp.sum(residual * residual), ('dom', 'blk'))  37.6 us
    all_to_all x2, blocking collectives, to_elements(): lax.all_to_all(buffer, ('dom', 'blk'), split_axis=1, concat_axis=1, tiled...  36.5 us
    dot_general x3, matrix products, local(): jnp.einsum('abe,cbe->cae', condensed, spread(direction), precision=PRECISE)  35.5 us
    unnamed x36, local copies, waits for them, and re-layouts  20 us
    scatter x4, local copies, waits for them, and re-layouts, assemble(): outgoing = jnp.zeros((mortar_values.shape[0], buffer_width + 1), jnp.floa...  17.1 us
  transfers between devices with their start and end apart: 4, of which 2 were waited for; matrix products, arithmetic and copies ran while one was open for 14% of the time, Pallas kernels for 0%

profile of v1, /device:TPU:1, one launch (start us, length us, event | category | flops | bytes accessed | tf_op | source)
XLA Modules:
  0.0 523.7 jit_solution(13813557679346247300)
XLA Ops:
  0.6 1.6 convert_reduce_fusion.3
  2.3 3.2 compare_select_fusion.2
  5.5 3.4 scatter_custom_fusion
  9.6 7.1 %all-to-all-start = ((s32[32,32,1]{1,2,0:T(1,128)}), s32[32,32,1]{1,2,0:T(1,128)S(1)}, u32[]{:S(2)}, u32[]{:S(2)}) async-start(s32[32,32,1]{1,2,0:T(1,128)} %bitcast.16), calls=%async_computation | async-start | bytes 32768 | tf_op jit(solution)/shard_map/all_to_all | solution.py:114
  18.4 5.1 copy.378
  23.5 4.5 copy.377
  28.0 8.5 %convolution_bitcast_fusion.14 = f32[3,64,128]{1,0,2:T(4,128)S(1)} fusion(f32[3,64,128]{1,0,2:T(4,128)S(1)} %copy.376, f32[64,64,128]{1,0,2:T(8,128)} %copy.377), kind=kOutput, calls=%fused_computation.55 | convolution fusion | flops 18874368 | bytes 2293760 | tf_op jit(solution)/shard_map/ike,cke->cie/dot_general | solution.py:142
  36.5 7.2 %fusion.54 = f32[128,96,64]{1,2,0:T(8,128)} fusion(f32[64,96,128]{1,0,2:T(8,128)S(1)} %copy-done, f32[64,64,128]{1,0,2:T(8,128)} %copy.377), kind=kOutput, calls=%fused_computation.135 | convolution fusion | flops 603979776 | bytes 8388608 | tf_op jit(solution)/shard_map/ike,kbe->ibe/dot_general | solution.py:145
  43.6 3.7 convolution_bitcast_fusion.13
  48.2 14.5 %fusion = f32[128,96,96]{2,1,0:T(8,128)} fusion(f32[64,96,128]{1,0,2:T(8,128)} %copy.378, f32[128,96,64]{1,2,0:T(8,128)} %fusion.54), kind=kOutput, calls=%fused_computation.18 | convolution fusion | flops 905969664 | bytes 11010048 | tf_op jit(solution)/shard_map/iae,ibe->abe/dot_general | solution.py:146
  64.3 4.3 scatter_custom_fusion.1
  69.8 6.3 %copy.393 = f32[128,96,96]{0,1,2:T(8,128)} copy(f32[128,96,96]{2,1,0:T(8,128)} %fusion) | data formatting | bytes 9437184 | tf_op jit(solution)/shard_map/iae,ibe->abe/dot_general | solution.py:146
  76.1 5.8 %all-to-all-start.1 = ((f32[32,1,1536]{2,1,0:T(1,128)}), f32[32,1,1536]{2,1,0:T(1,128)S(1)}, u32[]{:S(2)}, u32[]{:S(2)}) async-start(f32[32,1,1536]{2,1,0:T(1,128)} %reshape.401), calls=%async_computation.1 | async-start | bytes 393216 | tf_op jit(solution)/shard_map/all_to_all | solution.py:76
  83.3 7.9 %all-to-all-done.1 = f32[32,1,1536]{2,1,0:T(1,128)S(1)} async-done(((f32[32,1,1536]{2,1,0:T(1,128)}), f32[32,1,1536]{2,1,0:T(1,128)S(1)}, u32[]{:S(2)}, u32[]{:S(2)}) %all-to-all-start.1) | async-done | bytes 196640 | tf_op jit(solution)/shard_map/all_to_all | solution.py:76
  93.6 13.1 %scatter_custom_fusion.2 = f32[48,257]{0,1:T(8,128)S(1)} fusion(s32[1792]{0:T(1024)S(1)} %fusion.42, f32[1792,48]{1,0:T(8,128)S(1)} %copy.384, f32[]{:T(128)} %constant.68.clone.1), kind=kCustom, calls=%fused_computation.91 | custom fusion | flops 86016 | bytes 49348 | tf_op jit(solution)/shard_map/scatter-add | solution.py:131
  106.8 2.8 gather_fusion
  110.9 2.7 all-to-all-start.2
  113.5 7.0 %bitcast_add_fusion = f32[96,96,128]{2,1,0:T(8,128)} fusion(f32[96,96,128]{2,1,0:T(8,128)} %param.7, f32[128,96,96]{0,1,2:T(8,128)} %copy.393), kind=kLoop, calls=%fused_computation.17 | loop fusion | flops 1179648 | bytes 14155776 | tf_op jit(solution)/shard_map/add | solution.py:146
  120.5 6.3 %copy.395 = f32[96,96,128]{1,0,2:T(8,128)} copy(f32[96,96,128]{2,1,0:T(8,128)} %bitcast_add_fusion) | data formatting | bytes 9437184 | tf_op jit(solution)/shard_map/add | solution.py:146
  131.8 11.8 %convolution_bitcast_fusion.12 = f32[3,96,128]{1,0,2:T(4,128)S(1)} fusion(f32[3,96,128]{1,0,2:T(4,128)S(1)} %copy.394, f32[96,96,128]{1,0,2:T(8,128)} %copy.395), kind=kOutput, calls=%fused_computation.53 | convolution fusion | flops 42467328 | bytes 5013504 | tf_op jit(solution)/shard_map/abe,cbe->cae/dot_general | solution.py:152
  146.1 4.3 scatter_custom_fusion.3
  150.9 15.3 %all_to_all.105 = f32[32,1,1536]{2,1,0:T(1,128)S(1)} all-to-all(f32[32,1,1536]{2,1,0:T(1,128)S(1)} %reshape.405), channel_id=1, replica_groups=mesh['dom'=16,'blk'=2] {'dom','blk'}, dimensions={0} | all-to-all | bytes 393216 | tf_op jit(solution)/shard_map/all_to_all | solution.py:76
  168.0 13.1 %scatter_custom_fusion.4 = f32[48,257]{0,1:T(8,128)S(1)} fusion(s32[1792]{0:T(1024)S(1)} %fusion.42, f32[1792,48]{1,0:T(8,128)S(1)} %copy.401, f32[]{:T(128)} %constant.68.clone.1), kind=kCustom, calls=%fused_computation.88 | custom fusion | flops 86016 | bytes 49348 | tf_op jit(solution)/shard_map/scatter-add | solution.py:131
  181.9 37.6 %psum.97 = f32[]{:T(128)} all-reduce(f32[]{:T(128)} %get-tuple-element.23), channel_id=1, replica_groups=mesh['dom'=16,'blk'=2] {'dom','blk'}, use_global_device_ids=true, to_apply=%region_8.9 | all-reduce | flops 1 | bytes 8 | tf_op jit(solution)/shard_map/psum | solution.py:149
  219.5 4.1 all-reduce.6
  223.6 33.5 %all-reduce.4 = (f32[]{:T(128)}, f32[]{:T(128)}) all-reduce(f32[]{:T(128)} %get-tuple-element.36, f32[]{:T(128)} %get-tuple-element.37), channel_id=1, replica_groups=mesh['dom'=16,'blk'=2] {'dom'}, use_global_device_ids=true, to_apply=%region_13.14 | all-reduce | flops 2 | bytes 16 | tf_op jit(solution)/shard_map/psum | solution.py:154
  260.9 2.8 gather_fusion.2
  264.2 18.3 %all_to_all.106 = f32[32,1,1536]{2,1,0:T(1,128)S(1)} all-to-all(f32[32,1,1536]{2,1,0:T(1,128)S(1)} %reshape.407), channel_id=1, replica_groups=mesh['dom'=16,'blk'=2] {'dom','blk'}, dimensions={0} | all-to-all | bytes 393216 | tf_op jit(solution)/shard_map/all_to_all | solution.py:81
  287.4 11.8 %convolution_bitcast_fusion.11 = f32[3,96,128]{1,0,2:T(4,128)S(1)} fusion(f32[3,96,128]{1,0,2:T(4,128)S(1)} %copy.407, f32[96,96,128]{1,0,2:T(8,128)} %copy.395), kind=kOutput, calls=%fused_computation.52 | convolution fusion | flops 42467328 | bytes 5013504 | tf_op jit(solution)/shard_map/abe,cbe->cae/dot_general | solution.py:152
  301.7 4.3 scatter_custom_fusion.5
  306.5 11.5 %all_to_all.107 = f32[32,1,1536]{2,1,0:T(1,128)S(1)} all-to-all(f32[32,1,1536]{2,1,0:T(1,128)S(1)} %reshape.409), channel_id=1, replica_groups=mesh['dom'=16,'blk'=2] {'dom','blk'}, dimensions={0} | all-to-all | bytes 393216 | tf_op jit(solution)/shard_map/all_to_all | solution.py:76
  319.9 13.1 %scatter_custom_fusion.6 = f32[48,257]{0,1:T(8,128)S(1)} fusion(s32[1792]{0:T(1024)S(1)} %fusion.42, f32[1792,48]{1,0:T(8,128)S(1)} %copy.414, f32[]{:T(128)} %constant.68.clone.1), kind=kCustom, calls=%fused_computation.86 | custom fusion | flops 86016 | bytes 49348 | tf_op jit(solution)/shard_map/scatter-add | solution.py:131
  333.7 3.1 all-reduce.5
  336.9 31.9 %all-reduce.3 = (f32[]{:T(128)}, f32[]{:T(128)}, f32[]{:T(128)}) all-reduce(f32[]{:T(128)} %get-tuple-element.33, f32[]{:T(128)} %get-tuple-element.34, f32[]{:T(128)} %get-tuple-element.35), channel_id=1, replica_groups=mesh['dom'=16,'blk'=2] {'dom'}, use_global_device_ids=true, to_apply=%region_21.22 | all-reduce | flops 3 | bytes 24 | tf_op jit(solution)/shard_map/psum | solution.py:154
  370.9 2.8 gather_fusion.4
  374.2 18.2 %all_to_all.108 = f32[32,1,1536]{2,1,0:T(1,128)S(1)} all-to-all(f32[32,1,1536]{2,1,0:T(1,128)S(1)} %reshape.411), channel_id=1, replica_groups=mesh['dom'=16,'blk'=2] {'dom','blk'}, dimensions={0} | all-to-all | bytes 393216 | tf_op jit(solution)/shard_map/all_to_all | solution.py:81
  397.4 11.8 %convolution_bitcast_fusion.10 = f32[3,96,128]{1,0,2:T(4,128)S(1)} fusion(f32[3,96,128]{1,0,2:T(4,128)S(1)} %copy.420, f32[96,96,128]{1,0,2:T(8,128)} %copy.395), kind=kOutput, calls=%fused_computation.51 | convolution fusion | flops 42467328 | bytes 5013504 | tf_op jit(solution)/shard_map/abe,cbe->cae/dot_general | solution.py:152
  411.7 4.3 scatter_custom_fusion.7
  416.5 11.5 %all_to_all.109 = f32[32,1,1536]{2,1,0:T(1,128)S(1)} all-to-all(f32[32,1,1536]{2,1,0:T(1,128)S(1)} %reshape.413), channel_id=1, replica_groups=mesh['dom'=16,'blk'=2] {'dom','blk'}, dimensions={0} | all-to-all | bytes 393216 | tf_op jit(solution)/shard_map/all_to_all | solution.py:76
  429.9 13.1 %scatter_custom_fusion.8 = f32[48,257]{0,1:T(8,128)S(1)} fusion(s32[1792]{0:T(1024)S(1)} %fusion.42, f32[1792,48]{1,0:T(8,128)S(1)} %copy.427, f32[]{:T(128)} %constant.68.clone.1), kind=kCustom, calls=%fused_computation.84 | custom fusion | flops 86016 | bytes 49348 | tf_op jit(solution)/shard_map/scatter-add | solution.py:131
  443.7 3.1 psum.108
  446.8 31.9 %psum.109 = f32[]{:T(128)} all-reduce(f32[]{:T(128)} %psum.108), channel_id=1, replica_groups=mesh['dom'=16,'blk'=2] {'dom'}, use_global_device_ids=true, to_apply=%region_32.33 | all-reduce | flops 1 | bytes 8 | tf_op jit(solution)/shard_map/psum | solution.py:154
  479.4 2.8 gather_fusion.6
  483.4 9.7 %all-to-all-start.8 = ((f32[32,1,1536]{2,1,0:T(1,128)}), f32[32,1,1536]{2,1,0:T(1,128)S(1)}, u32[]{:S(2)}, u32[]{:S(2)}) async-start(f32[32,1,1536]{2,1,0:T(1,128)} %reshape.415), calls=%async_computation.8 | async-start | bytes 393216 | tf_op jit(solution)/shard_map/all_to_all | solution.py:81
  493.8 8.7 %all-to-all-done.8 = f32[32,1,1536]{2,1,0:T(1,128)S(1)} async-done(((f32[32,1,1536]{2,1,0:T(1,128)}), f32[32,1,1536]{2,1,0:T(1,128)S(1)}, u32[]{:S(2)}, u32[]{:S(2)}) %all-to-all-start.8) | async-done | bytes 196640 | tf_op jit(solution)/shard_map/all_to_all | solution.py:81
  503.9 1.6 gather_fusion.7
  507.5 8.5 %fusion.22 = f32[3,64,128]{1,0,2:T(4,128)S(1)} fusion(f32[3,64,128]{1,0,2:T(4,128)S(1)} %copy-done.4, f32[3,96,128]{1,0,2:T(4,128)S(1)} %copy.433, f32[64,96,128]{1,0,2:T(8,128)} %copy.378), kind=kOutput, calls=%fused_computation.50 | convolution fusion | flops 28336128 | bytes 3489792 | tf_op jit(solution)/shard_map/ibe,cbe->cie/dot_general | solution.py:175
  516.0 6.6 %convolution_bitcast_fusion.8 = f32[3,64,128]{1,0,2:T(4,128)S(1)} fusion(f32[3,64,128]{1,0,2:T(4,128)S(1)} %fusion.22, f32[64,64,128]{1,0,2:T(8,128)S(1)} %copy-done.1), kind=kOutput, calls=%fused_computation.48 | convolution fusion | flops 18874368 | bytes 2293760 | tf_op jit(solution)/shard_map/ike,cke->cie/dot_general | solution.py:176
  (132 shorter events, 49.4 us)
Async XLA Ops:
  0.6 22.9 %copy-start.5 = (f32[64,64,128]{2,1,0:T(8,128)S(1)}, f32[64,64,128]{2,1,0:T(8,128)}, u32[]{:S(2)}) copy-start(f32[64,64,128]{2,1,0:T(8,128)} %param.9) | copy-start | bytes 6291460
  9.6 66.6 %all-to-all-start = ((s32[32,32,1]{1,2,0:T(1,128)}), s32[32,32,1]{1,2,0:T(1,128)S(1)}, u32[]{:S(2)}, u32[]{:S(2)}) async-start(s32[32,32,1]{1,2,0:T(1,128)} %bitcast.16), calls=%async_computation | async-start | bytes 32768 | tf_op jit(solution)/shard_map/all_to_all | solution.py:114
  18.4 9.6 %copy-start.3 = (f32[3,64,128]{1,0,2:T(4,128)}, f32[3,64,128]{1,0,2:T(4,128)S(1)}, u32[]{:S(2)}) copy-start(f32[3,64,128]{1,0,2:T(4,128)S(1)} %copy.376) | copy-start | bytes 294916
  28.0 8.5 %copy-start = (f32[64,96,128]{1,0,2:T(8,128)S(1)}, f32[64,96,128]{1,0,2:T(8,128)}, u32[]{:S(2)}) copy-start(f32[64,96,128]{1,0,2:T(8,128)} %copy.378) | copy-start | bytes 9437188
  48.2 14.5 %copy-start.2 = (f32[5,16,16,1]{1,2,0,3:T(8,128)S(1)}, f32[5,16,16,1]{1,2,0,3:T(8,128)}, u32[]{:S(2)}) copy-start(f32[5,16,16,1]{1,2,0,3:T(8,128)} %constant.104) | copy-start | bytes 15364
  76.1 30.6 %copy-start.6 = (pred[257]{0:T(512)(128)(4,1)S(1)}, pred[257]{0:T(512)(128)(4,1)}, u32[]{:S(2)}) copy-start(pred[257]{0:T(512)(128)(4,1)} %constant.86.clone.1) | copy-start | bytes 775
  76.1 15.1 %all-to-all-start.1 = ((f32[32,1,1536]{2,1,0:T(1,128)}), f32[32,1,1536]{2,1,0:T(1,128)S(1)}, u32[]{:S(2)}, u32[]{:S(2)}) async-start(f32[32,1,1536]{2,1,0:T(1,128)} %reshape.401), calls=%async_computation.1 | async-start | bytes 393216 | tf_op jit(solution)/shard_map/all_to_all | solution.py:76
  110.9 15.9 %all-to-all-start.2 = ((f32[32,1,1536]{2,1,0:T(1,128)}), f32[32,1,1536]{2,1,0:T(1,128)S(1)}, u32[]{:S(2)}, u32[]{:S(2)}) async-start(f32[32,1,1536]{2,1,0:T(1,128)} %reshape.403), calls=%async_computation.2 | async-start | bytes 393216 | tf_op jit(solution)/shard_map/all_to_all | solution.py:81
  483.4 19.1 %all-to-all-start.8 = ((f32[32,1,1536]{2,1,0:T(1,128)}), f32[32,1,1536]{2,1,0:T(1,128)S(1)}, u32[]{:S(2)}, u32[]{:S(2)}) async-start(f32[32,1,1536]{2,1,0:T(1,128)} %reshape.415), calls=%async_computation.8 | async-start | bytes 393216 | tf_op jit(solution)/shard_map/all_to_all | solution.py:81
  503.9 3.6 copy-start.4
  507.5 8.5 %copy-start.1 = (f32[64,64,128]{1,0,2:T(8,128)S(1)}, f32[64,64,128]{1,0,2:T(8,128)}, u32[]{:S(2)}) copy-start(f32[64,64,128]{1,0,2:T(8,128)} %copy.377) | copy-start | bytes 6291460
